TPU v7x, 32 devices: a whole 2x2x4 slice. The times are simulated.
32 devices in a mesh: sens: 4 (over y, x), par: 8 (over z, core).
Axes of the slice: x: 2, y: 2, z: 4, core: 2. Of those that a mesh axis runs over, the one named last changes fastest.
Arguments:
- kernel: bfloat16 [2, 129, 64, 8192], P(None, None, 'sens', 'par'), may hold values from -0.0625 to 0.0625
- param: float32 [128, 2, 8192], P(None, None, 'par'), may hold values from -6 to 6
- observed: float32 [64, 128], P('sens'), may hold values from -6 to 6
- noise_scale: float32 [64], P('sens'), may hold values from 0.3 to 3
- robust_flags: int32 [64, 128], P('sens'), may hold values 0 or 1
- kappa_field: float32 [8192], P('par'), may hold values from 0.01 to 0.1
- coupling: float32 [8192], P('par'), may hold values from 0.05 to 0.2
- neighbours: int32 [8, 4], replicated, may hold values from -1 to 7, as said below
Outputs:
- gradient: float32 [128, 2, 8192], P(None, None, 'par')
- direction: float32 [128, 2, 8192], P(None, None, 'par')
Inputs may be any that keep to these rules, and one draw needn't show every extreme that they name: `neighbours`: row k lists the tiles west, east, south and north of tile k, or -1 where there is none; the tiles fill a grid of 2 columns and 4 rows in an order drawn from the seed, and the relations are mutual.
All inputs are finite; a program needn't handle non-finite values. No bound on the sum of `robust_flags` on one device may be relied on, other than what follows from the above.
Results may differ from a plain program's by a relative error of at most 0.003.
Values may be sent and summed in bfloat16 or wider, within the bound.
A program may use at most 128 MiB of HBM per device.

v0:
```python
import jax
import jax.numpy as jnp
from jax import lax
from jax.sharding import PartitionSpec as P

SWEEPS = 8
TSIDE = 32
huber_limit = 1.345


def tables(length):
    period = 2 * length
    frequency = jnp.arange(length + 1, dtype=jnp.int32)
    moment = jnp.arange(length, dtype=jnp.int32)
    phases = frequency[:, None] * moment[None, :] % period
    angles = phases.astype(jnp.float32) * (2.0 * jnp.pi / period)
    cosine = jnp.cos(angles)
    sines = jnp.sin(angles)
    forward = jnp.concatenate([cosine, -sines], 0)
    weight = (
        jnp.where((frequency == 0) | (frequency == length), 1.0, 2.0).astype(jnp.float32) / period
    )
    backward = jnp.concatenate([weight[:, None] * cosine, -weight[:, None] * sines], 0)
    return (forward, backward)


def residual_spectrum(predicted, observed, noise_scale, robust_flags, backward):
    length = observed.shape[1]
    sensor_count = predicted.shape[1]
    samples = predicted.shape[2]
    series = jnp.dot(
        backward.T, predicted.reshape(-1, sensor_count * samples), precision=lax.Precision.HIGHEST
    )
    series = series.reshape(length, sensor_count, samples)
    scaled = (series - observed.T[:, :, None]) / noise_scale[None, :, None]
    robust = jnp.where(
        robust_flags.T[:, :, None] == 1, jnp.clip(scaled, -huber_limit, huber_limit), scaled
    )
    weighted = robust / noise_scale[None, :, None]
    spectral = jnp.dot(backward, weighted.reshape(length, -1), precision=lax.Precision.HIGHEST)
    return spectral.reshape(-1, sensor_count, samples)


def neighbour_sum(values, own_row):
    row_count, cell_count = values.shape
    square = values.reshape(row_count, TSIDE, TSIDE)
    outgoing = jnp.stack([square[:, :, 0], square[:, :, -1], square[:, 0, :], square[:, -1, :]], 0)
    outgoing = outgoing.reshape(4, row_count * TSIDE)
    all_rims = lax.all_gather(outgoing.astype(jnp.bfloat16), "par", axis=0, tiled=True).astype(
        outgoing.dtype
    )

    def facing(tile, edge_index):
        picked = all_rims[jnp.maximum(tile, 0) * 4 + edge_index]
        return jnp.where(tile >= 0, picked, 0.0).reshape(row_count, TSIDE)

    west_rim = facing(own_row[0], 1)
    east_rim = facing(own_row[1], 0)
    south_rim = facing(own_row[2], 3)
    north_rim = facing(own_row[3], 2)
    column = jnp.arange(cell_count) % TSIDE
    zeros_column = jnp.zeros((row_count, 1), values.dtype)
    east_side = jnp.where(
        column == TSIDE - 1,
        jnp.repeat(east_rim, TSIDE, axis=1),
        jnp.concatenate([values[:, 1:], zeros_column], 1),
    )
    west_side = jnp.where(
        column == 0,
        jnp.repeat(west_rim, TSIDE, axis=1),
        jnp.concatenate([zeros_column, values[:, :-1]], 1),
    )
    north_side = jnp.concatenate([values[:, TSIDE:], north_rim], 1)
    south_side = jnp.concatenate([south_rim, values[:, :-TSIDE]], 1)
    return east_side + west_side + north_side + south_side


def per_device(
    kernel, param, observed, noise_scale, robust_flags, kappa_field, coupling, neighbours
):
    length, samples, cell_count = param.shape
    sensor_count = observed.shape[0]
    spectra_rows = 2 * (length + 1)
    forward, backward = tables(length)
    spectrum = jnp.dot(forward, param.reshape(length, -1), precision=lax.Precision.HIGHEST)
    spectrum = spectrum.reshape(2, length + 1, samples, cell_count).astype(jnp.bfloat16)
    product = jnp.einsum("ifsc,jfbc->ijfsb", kernel, spectrum, preferred_element_type=jnp.float32)
    partial_sum = jnp.concatenate([product[0, 0] - product[1, 1], product[0, 1] + product[1, 0]], 0)
    predicted = lax.psum(partial_sum, "par")
    adjoint = residual_spectrum(predicted, observed, noise_scale, robust_flags, backward).astype(
        jnp.bfloat16
    )
    adjoint = adjoint.reshape(2, length + 1, sensor_count, samples)
    back_product = jnp.einsum(
        "ifsc,jfsb->ijfbc", kernel, adjoint, preferred_element_type=jnp.float32
    )
    partial_grad = jnp.concatenate(
        [back_product[0, 0] + back_product[1, 1], back_product[0, 1] - back_product[1, 0]], 0
    )
    partial_grad = partial_grad.reshape(spectra_rows, samples * cell_count)
    row_block = length // lax.axis_size("sens")
    transposed = forward.T
    misfit = lax.psum_scatter(
        jnp.dot(transposed, partial_grad, precision=lax.Precision.HIGHEST),
        "sens",
        scatter_dimension=0,
        tiled=True,
    )
    field_rows = lax.dynamic_slice_in_dim(param, lax.axis_index("sens") * row_block, row_block, 0)
    block_length = field_rows.shape[0]
    flat_field = field_rows.reshape(-1, cell_count)
    misfit = misfit.reshape(-1, cell_count)
    diagonal = kappa_field + 4.0 * coupling
    own_row = neighbours[lax.axis_index("par")]
    gradient = misfit + diagonal * flat_field - coupling * neighbour_sum(flat_field, own_row)
    direction = gradient / diagonal
    for sweep in range(SWEEPS - 1):
        direction = (gradient + coupling * neighbour_sum(direction, own_row)) / diagonal
    gradient = gradient.reshape(block_length, samples, cell_count)
    direction = direction.reshape(block_length, samples, cell_count)
    return (
        lax.all_gather(gradient, "sens", axis=0, tiled=True),
        lax.all_gather(direction, "sens", axis=0, tiled=True),
    )


def solution(mesh):
    return jax.shard_map(
        per_device,
        mesh=mesh,
        in_specs=(
            P(None, None, "sens", "par"),
            P(None, None, "par"),
            P("sens", None),
            P("sens"),
            P("sens", None),
            P("par"),
            P("par"),
            P(),
        ),
        out_specs=(P(None, None, "par"), P(None, None, "par")),
        check_vma=False,
    )
```

profile of v0, /device:TPU:0, one launch (start us, length us, event | category | flops | bytes accessed | tf_op | source)
XLA Modules:
  0.0 279.7 jit_solution(1671266593527884040)
XLA Ops:
  7.6 1.6 copy.337
  9.5 1.9 fusion.11
  11.4 13.9 %fusion.12 = f32[2,2,129,16,2]{3,4,0,1,2:T(2,128)S(1)} fusion(bf16[2,129,2,1024,1]{3,1,2,0,4:T(8,128)(2,1)S(1)} %fusion.11, bf16[2,129,16,1024]{3,2,1,0:T(8,128)(2,1)} %param.8), kind=kOutput, calls=%fused_computation.11 | convolution fusion | flops 33816576 | bytes 9576960 | tf_op jit(solution)/shard_map/ifsc,jfbc->ijfsb/dot_general | solution.py:87
  25.9 30.7 %psum.7 = f32[16,2,258]{2,0,1:T(8,128)S(1)} all-reduce(f32[16,2,258]{2,0,1:T(8,128)S(1)} %copy.250), channel_id=1, replica_groups=mesh['sens'=4,'par'=8] {'par'}, use_global_device_ids=true, to_apply=%region_0.1 | all-reduce | flops 8256 | bytes 66048 | tf_op jit(solution)/shard_map/psum | solution.py:89
  58.1 5.4 %fusion.4 = f32[2,2,129,2,1024]{4,3,0,1,2:T(2,128)S(1)} fusion(bf16[2,129,16,2,1]{2,3,4,0,1:T(2,128)(2,1)S(1)} %copy.325, bf16[2,129,16,1024]{3,2,1,0:T(8,128)(2,1)} %param.8), kind=kOutput, calls=%fused_computation.4 | convolution fusion | flops 33816576 | bytes 12697728 | tf_op jit(solution)/shard_map/ifsc,jfsb->ijfbc/dot_general | solution.py:94
  63.5 1.1 fusion.17
  66.1 3.0 %fusion.7 = f32[128,2048]{1,0:T(8,128)} fusion(f32[258,128]{1,0:T(8,128)S(1)} %pad_maximum_fusion.1, f32[129,2048]{1,0:T(8,128)S(1)} %bitcast.187, f32[129,2048]{1,0:T(8,128)S(1)} %bitcast.186), kind=kOutput, calls=%fused_computation.5 | convolution fusion | flops 812126208 | bytes 3294208 | tf_op jit(solution)/shard_map/dot_general | solution.py:104
  75.3 1.1 fusion.121
  78.1 14.0 %all-gather = bf16[8,4,2048]{2,1,0:T(4,128)(2,1)S(1)} all-gather(bf16[1,4,2048]{2,1,0:T(4,128)(2,1)S(1)} %maximum_bitcast_fusion.7), channel_id=1, replica_groups=mesh['sens'=4,'par'=8] {'par'}, dimensions={0}, use_global_device_ids=true | all-gather | bytes 147456 | tf_op jit(solution)/shard_map/all_gather | solution.py:49
  93.6 1.9 reduce-scatter.2.cloned.1.call-done
  95.5 1.0 reshape.446
  98.2 14.3 %all-gather.1 = bf16[8,4,2048]{2,1,0:T(4,128)(2,1)S(1)} all-gather(bf16[1,4,2048]{2,1,0:T(4,128)(2,1)S(1)} %maximum_bitcast_fusion.8), channel_id=1, replica_groups=mesh['sens'=4,'par'=8] {'par'}, dimensions={0}, use_global_device_ids=true | all-gather | bytes 147456 | tf_op jit(solution)/shard_map/all_gather | solution.py:49
  115.1 14.0 %all-gather.2 = bf16[8,4,2048]{2,1,0:T(4,128)(2,1)S(1)} all-gather(bf16[1,4,2048]{2,1,0:T(4,128)(2,1)S(1)} %maximum_bitcast_fusion.9), channel_id=1, replica_groups=mesh['sens'=4,'par'=8] {'par'}, dimensions={0}, use_global_device_ids=true | all-gather | bytes 147456 | tf_op jit(solution)/shard_map/all_gather | solution.py:49
  131.8 14.0 %all-gather.3 = bf16[8,4,2048]{2,1,0:T(4,128)(2,1)S(1)} all-gather(bf16[1,4,2048]{2,1,0:T(4,128)(2,1)S(1)} %maximum_bitcast_fusion.10), channel_id=1, replica_groups=mesh['sens'=4,'par'=8] {'par'}, dimensions={0}, use_global_device_ids=true | all-gather | bytes 147456 | tf_op jit(solution)/shard_map/all_gather | solution.py:49
  148.4 14.0 %all-gather.4 = bf16[8,4,2048]{2,1,0:T(4,128)(2,1)S(1)} all-gather(bf16[1,4,2048]{2,1,0:T(4,128)(2,1)S(1)} %maximum_bitcast_fusion.11), channel_id=1, replica_groups=mesh['sens'=4,'par'=8] {'par'}, dimensions={0}, use_global_device_ids=true | all-gather | bytes 147456 | tf_op jit(solution)/shard_map/all_gather | solution.py:49
  165.0 14.0 %all-gather.5 = bf16[8,4,2048]{2,1,0:T(4,128)(2,1)S(1)} all-gather(bf16[1,4,2048]{2,1,0:T(4,128)(2,1)S(1)} %maximum_bitcast_fusion.12), channel_id=1, replica_groups=mesh['sens'=4,'par'=8] {'par'}, dimensions={0}, use_global_device_ids=true | all-gather | bytes 147456 | tf_op jit(solution)/shard_map/all_gather | solution.py:49
  181.6 14.0 %all-gather.6 = bf16[8,4,2048]{2,1,0:T(4,128)(2,1)S(1)} all-gather(bf16[1,4,2048]{2,1,0:T(4,128)(2,1)S(1)} %maximum_bitcast_fusion.13), channel_id=1, replica_groups=mesh['sens'=4,'par'=8] {'par'}, dimensions={0}, use_global_device_ids=true | all-gather | bytes 147456 | tf_op jit(solution)/shard_map/all_gather | solution.py:49
  198.3 14.0 %all-gather.7 = bf16[8,4,2048]{2,1,0:T(4,128)(2,1)S(1)} all-gather(bf16[1,4,2048]{2,1,0:T(4,128)(2,1)S(1)} %maximum_bitcast_fusion.14), channel_id=1, replica_groups=mesh['sens'=4,'par'=8] {'par'}, dimensions={0}, use_global_device_ids=true | all-gather | bytes 147456 | tf_op jit(solution)/shard_map/all_gather | solution.py:49
  213.5 0.8 reshape.472
  214.5 0.8 reshape.450
  215.3 25.6 %all-gather.13.cloned.1.call-done = f32[128,2,1024]{2,1,0:T(2,128)} async-done(((f32[32,2,1024]{2,1,0:T(2,128)}), f32[128,2,1024]{2,1,0:T(2,128)}) %all-gather.13.cloned.1.call-update) | async-done | bytes 1048592 | tf_op jit(solution)/shard_map/all_gather | solution.py:123
  240.9 28.9 %all-gather.11.cloned.1.call-done = f32[128,2,1024]{2,1,0:T(2,128)} async-done(((f32[32,2,1024]{2,1,0:T(2,128)}), f32[128,2,1024]{2,1,0:T(2,128)}) %all-gather.11.cloned.1.call-update) | async-done | bytes 1048592 | tf_op jit(solution)/shard_map/all_gather | solution.py:122
  269.9 2.3 copy.356
  272.2 1.0 copy.357
  (261 shorter events, 26.0 us)
Async XLA Ops:
  7.2 62.1 %copy-start = (s32[8,4]{0,1:T(4,128)S(1)}, s32[8,4]{0,1:T(4,128)}, u32[]{:S(2)}) copy-start(s32[8,4]{0,1:T(4,128)} %param.15) | copy-start | bytes 388
  7.2 88.3 %reduce-scatter.2.cloned.1.call-start = ((), (), s32[]{:S(2)}) async-start(), calls=%async_computation.1 | async-start | bytes 1310720 | tf_op jit(solution)/shard_map/reduce_scatter | solution.py:103
  25.3 31.9 %copy-start.3 = (s32[16,128]{1,0:T(8,128)S(1)}, s32[16,128]{1,0:T(8,128)}, u32[]{:S(2)}) copy-start(s32[16,128]{1,0:T(8,128)} %param.12) | copy-start | bytes 24580
  25.3 31.9 %copy-start.5 = (f32[16,128]{1,0:T(8,128)S(1)}, f32[16,128]{1,0:T(8,128)}, u32[]{:S(2)}) copy-start(f32[16,128]{1,0:T(8,128)} %param.10) | copy-start | bytes 24580
  25.3 31.9 %copy-start.6 = (f32[16]{0:T(128)S(1)}, f32[16]{0:T(128)}, u32[]{:S(2)}) copy-start(f32[16]{0:T(128)} %param.11) | copy-start | bytes 196
  69.2 171.7 %all-gather.13.cloned.1.call-start = ((), (), s32[]{:S(2)}) async-start(), calls=%async_computation.3 | async-start | bytes 1310720 | tf_op jit(solution)/shard_map/all_gather | solution.py:123
  92.6 0.8 copy-start.2
  92.6 0.8 copy-start.4
  214.4 55.5 %all-gather.11.cloned.1.call-start = ((), (), s32[]{:S(2)}) async-start(), calls=%async_computation.2 | async-start | bytes 1310720 | tf_op jit(solution)/shard_map/all_gather | solution.py:122
  240.9 31.2 %copy-start.1 = (f32[128,2,1024]{2,1,0:T(2,128)S(1)}, f32[128,2,1024]{2,1,0:T(2,128)}, u32[]{:S(2)}) copy-start(f32[128,2,1024]{2,1,0:T(2,128)} %all-gather.13.cloned.1.call-done) | copy-start | bytes 3145732
Sparse Core Ops, SparseCore 0:
  69.3 26.1 reduce-scatter.1
  214.5 26.3 all-gather.12
  243.4 26.4 all-gather.10
where the time goes:
time: 280 us
  blocking collectives  143 us (51%)
  waiting for transfers between devices  56.5 us (20%)
  local copies, waits for them, and re-layouts  28.3 us (10%)
  matrix products  24.8 us (9%)
  between operations  20.3 us (7%)
  other arithmetic  6.71 us (2%)
    all_gather x8, blocking collectives, neighbour_sum(): lax.all_gather(outgoing.astype(jnp.bfloat16), 'par', axis=0, tiled=True)  112 us
    psum x1, blocking collectives, per_device(): predicted = lax.psum(partial_sum, 'par')  30.7 us
    all_gather x1, waiting for transfers between devices, per_device(): lax.all_gather(gradient, 'sens', axis=0, tiled=True)  28.9 us
    all_gather x1, waiting for transfers between devices, per_device(): lax.all_gather(direction, 'sens', axis=0, tiled=True)  25.6 us
    dot_general x1, matrix products, per_device(): jnp.einsum('ifsc,jfbc->ijfsb', kernel, spectrum, preferred_element_type=j...  13.9 us
    unnamed x21, local copies, waits for them, and re-layouts  6.34 us
  transfers between devices with their start and end apart: 3, of which 3 were waited for; matrix products, arithmetic and copies ran while one was open for 2% of the time, Pallas kernels for 0%

commit v1 on v0

--- a/solution.py
+++ b/solution.py
@@ -86,7 +86,11 @@
     spectrum = spectrum.reshape(2, length + 1, samples, cell_count).astype(jnp.bfloat16)
     product = jnp.einsum("ifsc,jfbc->ijfsb", kernel, spectrum, preferred_element_type=jnp.float32)
     partial_sum = jnp.concatenate([product[0, 0] - product[1, 1], product[0, 1] + product[1, 0]], 0)
-    predicted = lax.psum(partial_sum, "par")
+    predicted = partial_sum
+    for hop in (1, 2, 4):
+        predicted = predicted + lax.ppermute(
+            predicted, "par", [(dev, dev ^ hop) for dev in range(8)]
+        )
     adjoint = residual_spectrum(predicted, observed, noise_scale, robust_flags, backward).astype(
         jnp.bfloat16
     )

time: 280 us -> 264 us (0.943)
  blocking collectives: 143 us -> 113 us
  waiting for transfers between devices: 56.5 us -> 64 us
  starting transfers between devices: 0.12 us -> 6.69 us
    psum x1 -> x0, blocking collectives: 30.7 us -> none  [per_device(): predicted = lax.psum(partial_sum, 'par')]
    ppermute x0 -> x3, starting transfers between devices: none -> 6.57 us  [per_device(): lax.ppermute(predicted, 'par', [(dev, dev ^ hop) for dev in range(8)])]
    ppermute x0 -> x3, waiting for transfers between devices: none -> 4.45 us  [per_device(): lax.ppermute(predicted, 'par', [(dev, dev ^ hop) for dev in range(8)])]
    reduce_scatter x1, waiting for transfers between devices: 1.89 us -> 5.02 us  [per_device(): lax.psum_scatter(jnp.dot(transposed, partial_grad, precision=lax.Precisio...]
  transfers between devices with their start and end apart: 3 -> 6, of which waited for: 3 -> 6; matrix products, arithmetic and copies ran while one was open for 2% -> 2% of each run, Pallas kernels for 0% -> 0%
where the time goes in v1:
time: 264 us
  blocking collectives  113 us (43%)
  waiting for transfers between devices  64 us (24%)
  local copies, waits for them, and re-layouts  28.3 us (11%)
  matrix products  25 us (9%)
  between operations  20.3 us (8%)
  starting transfers between devices  6.69 us (3%)
  other arithmetic  6.68 us (3%)
    all_gather x8, blocking collectives, neighbour_sum(): lax.all_gather(outgoing.astype(jnp.bfloat16), 'par', axis=0, tiled=True)  113 us
    all_gather x1, waiting for transfers between devices, per_device(): lax.all_gather(gradient, 'sens', axis=0, tiled=True)  28.9 us
    all_gather x1, waiting for transfers between devices, per_device(): lax.all_gather(direction, 'sens', axis=0, tiled=True)  25.6 us
    dot_general x1, matrix products, per_device(): jnp.einsum('ifsc,jfbc->ijfsb', kernel, spectrum, preferred_element_type=j...  13.9 us
    ppermute x3, starting transfers between devices, per_device(): lax.ppermute(predicted, 'par', [(dev, dev ^ hop) for dev in range(8)])  6.57 us
    unnamed x21, local copies, waits for them, and re-layouts  6.34 us
    dot_general x1, matrix products, per_device(): jnp.einsum('ifsc,jfsb->ijfbc', kernel, adjoint, preferred_element_type=jn...  5.6 us
  transfers between devices with their start and end apart: 6, of which 6 were waited for; matrix products, arithmetic and copies ran while one was open for 2% of the time, Pallas kernels for 0%

profile of v1, /device:TPU:0, one launch (start us, length us, event | category | flops | bytes accessed | tf_op | source)
XLA Modules:
  0.0 263.9 jit_solution(15968916491099985108)
XLA Ops:
  7.6 1.6 copy.257
  9.5 1.9 fusion.11
  11.4 13.9 %fusion.12 = f32[2,2,129,16,2]{3,4,0,1,2:T(2,128)S(1)} fusion(bf16[2,129,2,1024,1]{3,1,2,0,4:T(8,128)(2,1)S(1)} %fusion.11, bf16[2,129,16,1024]{3,2,1,0:T(8,128)(2,1)} %param.8), kind=kOutput, calls=%fused_computation.11 | convolution fusion | flops 33816576 | bytes 9576960 | tf_op jit(solution)/shard_map/ifsc,jfbc->ijfsb/dot_general | solution.py:87
  27.2 3.0 %collective-permute-start.1 = (f32[258,16,2]{0,1,2:T(8,128)S(1)}, f32[258,16,2]{0,1,2:T(8,128)S(1)}, u32[]{:S(2)}, u32[]{:S(2)}) collective-permute-start(f32[258,16,2]{0,1,2:T(8,128)S(1)} %add.320), channel_id=1, source_target_pairs={{0,2},{1,3},{2,0},{3,1},{4,6},{5,7},{6,4},{7,5},{8,10},{9,11},{10,... | collective-permute-start | bytes 99080 | tf_op jit(solution)/shard_map/ppermute | solution.py:91
  30.4 1.8 collective-permute-done.1
  32.2 3.1 %collective-permute-start.2 = (f32[258,16,2]{0,1,2:T(8,128)S(1)}, f32[258,16,2]{0,1,2:T(8,128)S(1)}, u32[]{:S(2)}, u32[]{:S(2)}) collective-permute-start(f32[258,16,2]{0,1,2:T(8,128)S(1)} %add.321), channel_id=1, source_target_pairs={{0,4},{1,5},{2,6},{3,7},{4,0},{5,1},{6,2},{7,3},{8,12},{9,13},{10,... | collective-permute-start | bytes 99080 | tf_op jit(solution)/shard_map/ppermute | solution.py:91
  35.4 2.1 collective-permute-done.2
  38.4 5.6 %fusion.4 = f32[2,2,129,2,1024]{4,3,0,1,2:T(2,128)S(1)} fusion(bf16[2,129,16,2,1]{2,3,4,0,1:T(2,128)(2,1)S(1)} %copy.247, bf16[2,129,16,1024]{3,2,1,0:T(8,128)(2,1)} %param.8), kind=kOutput, calls=%fused_computation.4 | convolution fusion | flops 33816576 | bytes 12697728 | tf_op jit(solution)/shard_map/ifsc,jfsb->ijfbc/dot_general | solution.py:98
  44.0 1.1 fusion.17
  46.6 3.0 %fusion.7 = f32[128,2048]{1,0:T(8,128)} fusion(f32[258,128]{1,0:T(8,128)S(1)} %pad_maximum_fusion, f32[129,2048]{1,0:T(8,128)S(1)} %bitcast.176, f32[129,2048]{1,0:T(8,128)S(1)} %bitcast.175), kind=kOutput, calls=%fused_computation.5 | convolution fusion | flops 812126208 | bytes 3294208 | tf_op jit(solution)/shard_map/dot_general | solution.py:108
  55.8 1.1 fusion.125
  58.5 14.6 %all-gather = bf16[8,4,2048]{2,1,0:T(4,128)(2,1)S(1)} all-gather(bf16[1,4,2048]{2,1,0:T(4,128)(2,1)S(1)} %maximum_bitcast_fusion.7), channel_id=1, replica_groups=mesh['sens'=4,'par'=8] {'par'}, dimensions={0}, use_global_device_ids=true | all-gather | bytes 147456 | tf_op jit(solution)/shard_map/all_gather | solution.py:49
  74.7 5.0 %reduce-scatter.2.cloned.1.call-done = f32[32,2048]{1,0:T(8,128)} async-done(((f32[128,2048]{1,0:T(8,128)}), f32[32,2048]{1,0:T(8,128)}) %reduce-scatter.2.cloned.1.call-update) | async-done | bytes 262160 | tf_op jit(solution)/shard_map/reduce_scatter | solution.py:107
  79.8 1.0 reshape.446
  82.4 14.1 %all-gather.1 = bf16[8,4,2048]{2,1,0:T(4,128)(2,1)S(1)} all-gather(bf16[1,4,2048]{2,1,0:T(4,128)(2,1)S(1)} %maximum_bitcast_fusion.8), channel_id=1, replica_groups=mesh['sens'=4,'par'=8] {'par'}, dimensions={0}, use_global_device_ids=true | all-gather | bytes 147456 | tf_op jit(solution)/shard_map/all_gather | solution.py:49
  99.2 14.2 %all-gather.2 = bf16[8,4,2048]{2,1,0:T(4,128)(2,1)S(1)} all-gather(bf16[1,4,2048]{2,1,0:T(4,128)(2,1)S(1)} %maximum_bitcast_fusion.9), channel_id=1, replica_groups=mesh['sens'=4,'par'=8] {'par'}, dimensions={0}, use_global_device_ids=true | all-gather | bytes 147456 | tf_op jit(solution)/shard_map/all_gather | solution.py:49
  116.0 14.0 %all-gather.3 = bf16[8,4,2048]{2,1,0:T(4,128)(2,1)S(1)} all-gather(bf16[1,4,2048]{2,1,0:T(4,128)(2,1)S(1)} %maximum_bitcast_fusion.10), channel_id=1, replica_groups=mesh['sens'=4,'par'=8] {'par'}, dimensions={0}, use_global_device_ids=true | all-gather | bytes 147456 | tf_op jit(solution)/shard_map/all_gather | solution.py:49
  132.7 14.0 %all-gather.4 = bf16[8,4,2048]{2,1,0:T(4,128)(2,1)S(1)} all-gather(bf16[1,4,2048]{2,1,0:T(4,128)(2,1)S(1)} %maximum_bitcast_fusion.11), channel_id=1, replica_groups=mesh['sens'=4,'par'=8] {'par'}, dimensions={0}, use_global_device_ids=true | all-gather | bytes 147456 | tf_op jit(solution)/shard_map/all_gather | solution.py:49
  149.3 14.0 %all-gather.5 = bf16[8,4,2048]{2,1,0:T(4,128)(2,1)S(1)} all-gather(bf16[1,4,2048]{2,1,0:T(4,128)(2,1)S(1)} %maximum_bitcast_fusion.12), channel_id=1, replica_groups=mesh['sens'=4,'par'=8] {'par'}, dimensions={0}, use_global_device_ids=true | all-gather | bytes 147456 | tf_op jit(solution)/shard_map/all_gather | solution.py:49
  165.9 14.0 %all-gather.6 = bf16[8,4,2048]{2,1,0:T(4,128)(2,1)S(1)} all-gather(bf16[1,4,2048]{2,1,0:T(4,128)(2,1)S(1)} %maximum_bitcast_fusion.13), channel_id=1, replica_groups=mesh['sens'=4,'par'=8] {'par'}, dimensions={0}, use_global_device_ids=true | all-gather | bytes 147456 | tf_op jit(solution)/shard_map/all_gather | solution.py:49
  182.5 14.0 %all-gather.7 = bf16[8,4,2048]{2,1,0:T(4,128)(2,1)S(1)} all-gather(bf16[1,4,2048]{2,1,0:T(4,128)(2,1)S(1)} %maximum_bitcast_fusion.14), channel_id=1, replica_groups=mesh['sens'=4,'par'=8] {'par'}, dimensions={0}, use_global_device_ids=true | all-gather | bytes 147456 | tf_op jit(solution)/shard_map/all_gather | solution.py:49
  199.6 25.6 %all-gather.13.cloned.1.call-done = f32[128,2,1024]{2,1,0:T(2,128)} async-done(((f32[32,2,1024]{2,1,0:T(2,128)}), f32[128,2,1024]{2,1,0:T(2,128)}) %all-gather.13.cloned.1.call-update) | async-done | bytes 1048592 | tf_op jit(solution)/shard_map/all_gather | solution.py:127
  225.2 28.9 %all-gather.11.cloned.1.call-done = f32[128,2,1024]{2,1,0:T(2,128)} async-done(((f32[32,2,1024]{2,1,0:T(2,128)}), f32[128,2,1024]{2,1,0:T(2,128)}) %all-gather.11.cloned.1.call-update) | async-done | bytes 1048592 | tf_op jit(solution)/shard_map/all_gather | solution.py:126
  254.1 2.3 copy.282
  (269 shorter events, 29.8 us)
Async XLA Ops:
  7.2 42.6 %copy-start = (s32[8,4]{0,1:T(4,128)S(1)}, s32[8,4]{0,1:T(4,128)}, u32[]{:S(2)}) copy-start(s32[8,4]{0,1:T(4,128)} %param.15) | copy-start | bytes 388
  7.2 72.6 %reduce-scatter.2.cloned.1.call-start = ((), (), s32[]{:S(2)}) async-start(), calls=%async_computation.1 | async-start | bytes 1310720 | tf_op jit(solution)/shard_map/reduce_scatter | solution.py:107
  25.3 10.0 %copy-start.3 = (s32[16,128]{1,0:T(8,128)S(1)}, s32[16,128]{1,0:T(8,128)}, u32[]{:S(2)}) copy-start(s32[16,128]{1,0:T(8,128)} %param.12) | copy-start | bytes 24580
  25.3 12.2 %copy-start.5 = (f32[16,128]{1,0:T(8,128)S(1)}, f32[16,128]{1,0:T(8,128)}, u32[]{:S(2)}) copy-start(f32[16,128]{1,0:T(8,128)} %param.10) | copy-start | bytes 24580
  25.3 12.2 %copy-start.6 = (f32[16]{0:T(128)S(1)}, f32[16]{0:T(128)}, u32[]{:S(2)}) copy-start(f32[16]{0:T(128)} %param.11) | copy-start | bytes 196
  25.8 1.4 collective-permute-start
  27.2 5.0 %collective-permute-start.1 = (f32[258,16,2]{0,1,2:T(8,128)S(1)}, f32[258,16,2]{0,1,2:T(8,128)S(1)}, u32[]{:S(2)}, u32[]{:S(2)}) collective-permute-start(f32[258,16,2]{0,1,2:T(8,128)S(1)} %add.320), channel_id=1, source_target_pairs={{0,2},{1,3},{2,0},{3,1},{4,6},{5,7},{6,4},{7,5},{8,10},{9,11},{10,... | collective-permute-start | bytes 99080 | tf_op jit(solution)/shard_map/ppermute | solution.py:91
  32.2 5.2 %collective-permute-start.2 = (f32[258,16,2]{0,1,2:T(8,128)S(1)}, f32[258,16,2]{0,1,2:T(8,128)S(1)}, u32[]{:S(2)}, u32[]{:S(2)}) collective-permute-start(f32[258,16,2]{0,1,2:T(8,128)S(1)} %add.321), channel_id=1, source_target_pairs={{0,4},{1,5},{2,6},{3,7},{4,0},{5,1},{6,2},{7,3},{8,12},{9,13},{10,... | collective-permute-start | bytes 99080 | tf_op jit(solution)/shard_map/ppermute | solution.py:91
  49.7 175.5 %all-gather.13.cloned.1.call-start = ((), (), s32[]{:S(2)}) async-start(), calls=%async_computation.3 | async-start | bytes 1310720 | tf_op jit(solution)/shard_map/all_gather | solution.py:127
  73.7 0.8 copy-start.2
  73.7 0.8 copy-start.4
  198.7 55.5 %all-gather.11.cloned.1.call-start = ((), (), s32[]{:S(2)}) async-start(), calls=%async_computation.2 | async-start | bytes 1310720 | tf_op jit(solution)/shard_map/all_gather | solution.py:126
  225.2 31.2 %copy-start.1 = (f32[128,2,1024]{2,1,0:T(2,128)S(1)}, f32[128,2,1024]{2,1,0:T(2,128)}, u32[]{:S(2)}) copy-start(f32[128,2,1024]{2,1,0:T(2,128)} %all-gather.13.cloned.1.call-done) | copy-start | bytes 3145732
Sparse Core Ops, SparseCore 0:
  49.8 29.9 reduce-scatter.1
  198.8 26.3 all-gather.12
  227.6 26.4 all-gather.10
